TPU v7x, 32 devices: a whole 2x2x4 slice. The times are simulated.
32 devices in a mesh: dp: 4 (over z), mp: 8 (over y, x, core).
Axes of the slice: x: 2, y: 2, z: 4, core: 2. Of those that a mesh axis runs over, the one named last changes fastest.
Arguments:
- patches: bfloat16 [32, 256, 1152], P('dp'), may hold values from -6 to 6
- condition: bfloat16 [32, 1152], P('dp'), may hold values from -6 to 6
- lengths: int32 [32], P('dp'), may hold values from 144 to 192, as said below
- keep_order: int32 [32, 256], P('dp'), may hold values from 0 to 255, each once within a row
- cotangent: bfloat16 [32, 192, 1152], P('dp'), may hold values from -6 to 6
- projection_weight: bfloat16 [3, 1152, 1152], P(None, None, 'mp'), may hold values from -0.1875 to 0.1875
- query_value_bias: bfloat16 [2, 1152], P(None, 'mp'), may hold values from -3 to 3
- merge_weight: bfloat16 [1152, 1152], P('mp'), may hold values from -0.75 to 0.75
- merge_output_bias: bfloat16 [1152], replicated, may hold values from -3 to 3
- up_weight: bfloat16 [1152, 4608], P(None, 'mp'), may hold values from -0.1875 to 0.1875
- up_projection_bias: bfloat16 [4608], P('mp'), may hold values from -3 to 3
- down_weight: bfloat16 [4608, 1152], P('mp'), may hold values from -0.09375 to 0.09375
- down_projection_bias: bfloat16 [1152], replicated, may hold values from -3 to 3
- w_modulate: bfloat16 [1152, 6912], P(None, 'mp'), may hold values from -0.1875 to 0.1875
- bias_modulate: bfloat16 [6912], P('mp'), may hold values from -3 to 3
- bias_table: bfloat16 [16, 961], P('mp'), may hold values from -5 to 5
Outputs:
- block_out: bfloat16 [32, 192, 1152], P('dp')
- patch_grad: float32 [32, 256, 1152], P('dp')
- project_grad: float32 [3, 1152, 1152], P(None, None, 'mp')
- project_bias_grad: float32 [2, 1152], P(None, 'mp')
- merge_grad: float32 [1152, 1152], P('mp')
- merge_bias_grad: float32 [1152], replicated
- up_grad: float32 [1152, 4608], P(None, 'mp')
- up_bias_grad: float32 [4608], P('mp')
- down_grad: float32 [4608, 1152], P('mp')
- down_bias_grad: float32 [1152], replicated
- modulate_grad: float32 [1152, 6912], P(None, 'mp')
- modulate_bias_grad: float32 [6912], P('mp')
- table_grad: float32 [16, 961], P('mp')
Inputs may be any that keep to these rules, and one draw needn't show every extreme that they name: `lengths`: some sample keeps exactly 192 tokens. Each row holds every patch position once; slot j of sample b holds patch keep_order[b, j] when j < lengths[b].
All inputs are finite; a program needn't handle non-finite values.
Results may differ from a plain program's by a relative error of at most 0.02.
The roundings to bfloat16 on the way count: a program that leaves them out, or rounds other values in their place, can miss the bound.
Values may be sent and summed in bfloat16 or wider, within the bound.
A program may use at most 256 MiB of HBM per device.

v0:
```python
import math
import jax
import jax.numpy as jnp
from jax import lax
from jax.sharding import PartitionSpec as P

EXACT_PRECISION = lax.Precision.HIGHEST
EPSILON = 1e-06
MASKED = -1000000000.0


def layer_stats(values):
    centre = jnp.mean(values, axis=-1, keepdims=True)
    shifted = values - centre
    spread = jnp.mean(shifted * shifted, axis=-1, keepdims=True)
    inv_std = lax.rsqrt(spread + EPSILON)
    return (shifted * inv_std, inv_std)


def layer_back(gradient, normed, inv_std):
    mean_grad = jnp.mean(gradient, axis=-1, keepdims=True)
    mean_mix = jnp.mean(gradient * normed, axis=-1, keepdims=True)
    return inv_std * (gradient - mean_grad - normed * mean_mix)


def times_transposed(left_side, right_side):
    return lax.dot_general(
        left_side, right_side, (((1,), (1,)), ((), ())), preferred_element_type=jnp.float32
    )


def transposed_times(left_side, right_side):
    return lax.dot_general(
        left_side, right_side, (((0,), (0,)), ((), ())), preferred_element_type=jnp.float32
    )


def shift_onehot(grid_side):
    offsets = jnp.arange(grid_side, dtype=jnp.int32)
    targets = jnp.arange(2 * grid_side - 1, dtype=jnp.int32)
    return (
        offsets[:, None, None] - offsets[None, :, None] + grid_side - 1 == targets[None, None, :]
    ).astype(jnp.float32)


def body(
    patches,
    condition,
    lengths,
    keep_order,
    cotangent,
    projection_weight,
    query_value_bias,
    merge_weight,
    merge_output_bias,
    up_weight,
    up_projection_bias,
    down_weight,
    down_projection_bias,
    w_modulate,
    bias_modulate,
    bias_table,
):
    samples, patch_count, model_width = patches.shape
    keep_slots = cotangent.shape[1]
    grid_side = math.isqrt(patch_count)
    bucket_span = 2 * grid_side - 1
    heads_here = bias_table.shape[0]
    local_width = projection_weight.shape[2]
    head_size = local_width // heads_here
    row_count = samples * keep_slots
    factor = head_size ** (-0.5)
    head_shape = (samples, keep_slots, heads_here, head_size)
    slot_ids = jnp.arange(keep_slots, dtype=jnp.int32)
    live_slots = (slot_ids[None, :] < lengths[:, None]).astype(jnp.float32)
    live_rows = live_slots.reshape(row_count, 1)
    positions = keep_order[:, :keep_slots]
    row_picker = (
        positions[:, :, None] == jnp.arange(patch_count, dtype=jnp.int32)[None, None, :]
    ).astype(jnp.float32) * live_slots[:, :, None]
    signal = jax.nn.silu(condition.astype(jnp.float32)).astype(jnp.bfloat16)
    local_mod = jnp.dot(
        signal, w_modulate, preferred_element_type=jnp.float32
    ) + bias_modulate.astype(jnp.float32)
    modulation = lax.all_gather(local_mod, "mp", axis=1, tiled=True)
    row_mod = jnp.broadcast_to(
        modulation[:, None, :], (samples, keep_slots, modulation.shape[1])
    ).reshape(row_count, modulation.shape[1])
    shift_one, scale_one, gate_one, shift_two, scale_two, gate_two = [
        row_mod[:, column * model_width : (column + 1) * model_width] for column in range(6)
    ]
    taken = jnp.take_along_axis(patches, positions[:, :, None], axis=1).astype(jnp.float32)
    retained_rows = (taken * live_slots[:, :, None]).reshape(row_count, model_width)
    normed_one, inv_one = layer_stats(retained_rows)
    attention_entry = (normed_one * (1.0 + scale_one) + shift_one).astype(jnp.bfloat16)
    projected = jnp.einsum(
        "rd,cde->cre", attention_entry, projection_weight, preferred_element_type=jnp.float32
    )
    bias_float = query_value_bias.astype(jnp.float32)
    query_heads = (projected[0] + bias_float[0]).astype(jnp.bfloat16).reshape(head_shape)
    key_heads = projected[1].astype(jnp.bfloat16).reshape(head_shape)
    value_heads = (projected[2] + bias_float[1]).astype(jnp.bfloat16).reshape(head_shape)
    spread_table = shift_onehot(grid_side)
    table_grid = bias_table.astype(jnp.float32).reshape(heads_here, bucket_span, bucket_span)
    grid_bias = jnp.einsum(
        "rsa,cdb,hab->hrcsd", spread_table, spread_table, table_grid, precision=EXACT_PRECISION
    ).reshape(heads_here, patch_count, patch_count)
    left_bias = jnp.einsum("sql,hlm->shqm", row_picker, grid_bias, precision=EXACT_PRECISION)
    pair_bias = jnp.einsum("shqm,skm->shqk", left_bias, row_picker, precision=EXACT_PRECISION)

    def attention_scores(query_part, key_part):
        logits = (
            jnp.einsum("sqhe,skhe->shqk", query_part, key_part, preferred_element_type=jnp.float32)
            * factor
        )
        return jnp.where(live_slots[:, None, None, :] > 0.5, logits + pair_bias, MASKED)

    scores = attention_scores(query_heads, key_heads)
    row_max = jnp.max(scores, axis=-1, keepdims=True)
    exponent = jnp.exp(scores - row_max)
    row_sum = jnp.sum(exponent, axis=-1, keepdims=True)
    log_total = row_max + jnp.log(row_sum)
    attended_values = jnp.einsum(
        "shqk,skhe->sqhe",
        (exponent / row_sum).astype(jnp.bfloat16),
        value_heads,
        preferred_element_type=jnp.float32,
    )
    attended_values = attended_values.reshape(row_count, local_width).astype(jnp.bfloat16)
    attn_sum = lax.psum(
        jnp.dot(attended_values, merge_weight, preferred_element_type=jnp.float32).astype(
            jnp.bfloat16
        ),
        "mp",
    ).astype(jnp.float32)
    attention_result = attn_sum + merge_output_bias.astype(jnp.float32)
    hidden_one = retained_rows + gate_one * attention_result
    normed_two, inv_two = layer_stats(hidden_one)
    mlp_own = (normed_two * (1.0 + scale_two) + shift_two).astype(jnp.bfloat16)
    preactivation_hidden = jnp.dot(
        mlp_own, up_weight, preferred_element_type=jnp.float32
    ) + up_projection_bias.astype(jnp.float32)
    activated_hidden = jax.nn.gelu(preactivation_hidden, approximate=True).astype(jnp.bfloat16)
    mlp_sum = lax.psum(
        jnp.dot(activated_hidden, down_weight, preferred_element_type=jnp.float32).astype(
            jnp.bfloat16
        ),
        "mp",
    ).astype(jnp.float32)
    feedforward_result = mlp_sum + down_projection_bias.astype(jnp.float32)
    out_own = ((hidden_one + gate_two * feedforward_result) * live_rows).astype(jnp.bfloat16)
    block_out = out_own.reshape(samples, keep_slots, model_width)
    d_out = cotangent.reshape(row_count, model_width).astype(jnp.float32) * live_rows
    d_mlp = (gate_two * d_out).astype(jnp.bfloat16)
    down_grad = transposed_times(activated_hidden, d_mlp)
    down_bias_grad = jnp.sum(d_mlp.astype(jnp.float32), axis=0)
    d_act = times_transposed(d_mlp, down_weight)
    gelu_pull = jax.vjp(
        lambda pre_value: jax.nn.gelu(pre_value, approximate=True), preactivation_hidden
    )[1]
    d_pre = gelu_pull(d_act)[0].astype(jnp.bfloat16)
    up_grad = transposed_times(mlp_own, d_pre)
    up_bias_grad = jnp.sum(d_pre.astype(jnp.float32), axis=0)
    d_mlp_in = lax.psum(times_transposed(d_pre, up_weight).astype(jnp.bfloat16), "mp").astype(
        jnp.float32
    )
    d_hidden_one = d_out + layer_back(d_mlp_in * (1.0 + scale_two), normed_two, inv_two)
    d_attn_own = (gate_one * d_hidden_one).astype(jnp.bfloat16)
    merge_grad = transposed_times(attended_values, d_attn_own)
    merge_bias_grad = jnp.sum(d_attn_own.astype(jnp.float32), axis=0)
    d_attended = times_transposed(d_attn_own, merge_weight).astype(jnp.bfloat16).reshape(head_shape)
    probs_back = jnp.exp(attention_scores(query_heads, key_heads) - log_total)
    d_probs = jnp.einsum(
        "sqhe,skhe->shqk", d_attended, value_heads, preferred_element_type=jnp.float32
    )
    d_values = jnp.einsum(
        "shqk,sqhe->skhe",
        probs_back.astype(jnp.bfloat16),
        d_attended,
        preferred_element_type=jnp.float32,
    ).astype(jnp.bfloat16)
    d_scores = probs_back * (d_probs - jnp.sum(probs_back * d_probs, axis=-1, keepdims=True))
    d_logits = d_scores.astype(jnp.bfloat16)
    d_queries = (
        jnp.einsum("shqk,skhe->sqhe", d_logits, key_heads, preferred_element_type=jnp.float32)
        * factor
    ).astype(jnp.bfloat16)
    d_keys = (
        jnp.einsum("shqk,sqhe->skhe", d_logits, query_heads, preferred_element_type=jnp.float32)
        * factor
    ).astype(jnp.bfloat16)
    left_grad = jnp.einsum("sqm,shqk->shmk", row_picker, d_scores, precision=EXACT_PRECISION)
    grid_grad = jnp.einsum("shmk,skn->hmn", left_grad, row_picker, precision=EXACT_PRECISION)
    grid_grad = grid_grad.reshape(heads_here, grid_side, grid_side, grid_side, grid_side)
    table_grad = jnp.einsum(
        "rsa,cdb,hrcsd->hab", spread_table, spread_table, grid_grad, precision=EXACT_PRECISION
    ).reshape(heads_here, bucket_span * bucket_span)
    d_projected = jnp.stack(
        [
            d_queries.reshape(row_count, local_width),
            d_keys.reshape(row_count, local_width),
            d_values.reshape(row_count, local_width),
        ]
    )
    project_grad = jnp.einsum(
        "rd,cre->cde", attention_entry, d_projected, preferred_element_type=jnp.float32
    )
    project_bias_grad = jnp.stack(
        [
            jnp.sum(d_projected[0].astype(jnp.float32), axis=0),
            jnp.sum(d_projected[2].astype(jnp.float32), axis=0),
        ]
    )
    d_attn_in = lax.psum(
        jnp.einsum(
            "cre,cde->rd", d_projected, projection_weight, preferred_element_type=jnp.float32
        ).astype(jnp.bfloat16),
        "mp",
    ).astype(jnp.float32)
    d_kept_own = d_hidden_one + layer_back(d_attn_in * (1.0 + scale_one), normed_one, inv_one)
    mod_rows = jnp.concatenate(
        [
            d_attn_in,
            d_attn_in * normed_one,
            d_hidden_one * attention_result,
            d_mlp_in,
            d_mlp_in * normed_two,
            feedforward_result * d_out,
        ],
        axis=1,
    )
    d_modulation = jnp.sum(mod_rows.reshape(samples, keep_slots, mod_rows.shape[1]), axis=1)
    live_grad = d_kept_own.reshape(samples, keep_slots, model_width) * live_slots[:, :, None]
    sample_ids = jnp.arange(samples, dtype=jnp.int32)[:, None]
    patch_grad = (
        jnp.zeros((samples, patch_count, model_width), jnp.float32)
        .at[sample_ids, positions]
        .add(live_grad)
    )
    modulate_cols = w_modulate.shape[1]
    own_modulation = lax.dynamic_slice_in_dim(
        d_modulation, lax.axis_index("mp") * modulate_cols, modulate_cols, 1
    )
    modulate_grad = jnp.dot(signal.astype(jnp.float32).T, own_modulation, precision=EXACT_PRECISION)
    modulate_bias_grad = jnp.sum(own_modulation, axis=0)
    (
        project_grad,
        project_bias_grad,
        merge_grad,
        merge_bias_grad,
        up_grad,
        up_bias_grad,
        down_grad,
        down_bias_grad,
        modulate_grad,
        modulate_bias_grad,
        table_grad,
    ) = (
        lax.psum(project_grad.astype(jnp.bfloat16), "dp").astype(jnp.float32),
        lax.psum(project_bias_grad.astype(jnp.bfloat16), "dp").astype(jnp.float32),
        lax.psum(merge_grad.astype(jnp.bfloat16), "dp").astype(jnp.float32),
        lax.psum(merge_bias_grad.astype(jnp.bfloat16), "dp").astype(jnp.float32),
        lax.psum(up_grad.astype(jnp.bfloat16), "dp").astype(jnp.float32),
        lax.psum(up_bias_grad.astype(jnp.bfloat16), "dp").astype(jnp.float32),
        lax.psum(down_grad.astype(jnp.bfloat16), "dp").astype(jnp.float32),
        lax.psum(down_bias_grad.astype(jnp.bfloat16), "dp").astype(jnp.float32),
        lax.psum(modulate_grad.astype(jnp.bfloat16), "dp").astype(jnp.float32),
        lax.psum(modulate_bias_grad.astype(jnp.bfloat16), "dp").astype(jnp.float32),
        lax.psum(table_grad.astype(jnp.bfloat16), "dp").astype(jnp.float32),
    )
    return (
        block_out,
        patch_grad,
        project_grad,
        project_bias_grad,
        merge_grad,
        merge_bias_grad,
        up_grad,
        up_bias_grad,
        down_grad,
        down_bias_grad,
        modulate_grad,
        modulate_bias_grad,
        table_grad,
    )


def solution(mesh):
    placed = (
        P("dp", None, None),
        P("dp", None),
        P("dp"),
        P("dp", None),
        P("dp", None, None),
        P(None, None, "mp"),
        P(None, "mp"),
        P("mp", None),
        P(),
        P(None, "mp"),
        P("mp"),
        P("mp", None),
        P(),
        P(None, "mp"),
        P("mp"),
        P("mp", None),
    )
    return jax.shard_map(
        body,
        mesh=mesh,
        in_specs=placed,
        out_specs=(
            P("dp", None, None),
            P("dp", None, None),
            P(None, None, "mp"),
            P(None, "mp"),
            P("mp", None),
            P(),
            P(None, "mp"),
            P("mp"),
            P("mp", None),
            P(),
            P(None, "mp"),
            P("mp"),
            P("mp", None),
        ),
        check_vma=False,
    )
```

profile of v0, /device:TPU:0, one launch (start us, length us, event | category | flops | bytes accessed | tf_op | source)
XLA Modules:
  0.0 739.9 jit_solution(1977281370888989965)
XLA Ops:
  10.4 32.2 %gather_fusion = bf16[1536,1152]{1,0:T(8,128)(2,1)} fusion(bf16[8,256,1152]{2,1,0:T(8,128)(2,1)} %param.16, s32[1536]{0:T(1024)S(1)} %reshape.282), kind=kCustom, calls=%fused_computation | custom fusion | bytes 7090176 | tf_op jit(solution)/shard_map/jit(take_along_axis)/gather | solution.py:92
  48.2 10.8 %all-gather = f32[8,864,8]{1,2,0:T(8,128)S(1)} all-gather(f32[1,864,8]{1,2,0:T(8,128)S(1)} %fusion.58), channel_id=1, replica_groups=mesh['dp'=4,'mp'=8] {'mp'}, dimensions={0}, use_global_device_ids=true | all-gather | bytes 248832 | tf_op jit(solution)/shard_map/all_gather | solution.py:85
  59.3 14.3 %broadcast_in_dim.39 = f32[8,192,6912]{2,1,0:T(8,128)} broadcast(f32[8,6912]{1,0:T(8,128)S(1)} %bitcast.184), dimensions={0,2} | broadcast | bytes 42688512 | tf_op jit(solution)/shard_map/broadcast_in_dim | solution.py:86
  73.6 6.7 fusion.4
  94.2 4.4 fusion.24
  109.8 5.5 fusion.111
  117.1 4.3 fusion.123
  121.3 62.6 %all-reduce.8.cloned.1.call-done = bf16[1536,1152]{1,0:T(8,128)(2,1)} async-done(((bf16[1536,1152]{1,0:T(8,128)(2,1)}), bf16[1536,1152]{1,0:T(8,128)(2,1)}) %all-reduce.8.cloned.1.call-update) | async-done | bytes 3538960 | tf_op jit(solution)/shard_map/psum | solution.py:130
  184.0 6.5 fusion.117
  193.5 6.1 fusion.3
  199.9 5.6 fusion.113
  206.7 4.7 convolution_convert_fusion.1
  211.9 7.6 %convolution_convert_fusion.2 = bf16[1536,1152]{1,0:T(8,128)(2,1)} fusion(bf16[576,1152]{1,0:T(8,128)(2,1)} %param.27, f32[1536,576]{0,1:T(8,128)} %get-tuple-element.52), kind=kOutput, calls=%fused_computation.12 | convolution fusion | flops 2048163840 | bytes 8404992 | tf_op jit(solution)/shard_map/dot_general | solution.py:145
  219.5 65.9 %all-reduce.10.cloned.1.call-done = bf16[1536,1152]{1,0:T(8,128)(2,1)} async-done(((bf16[1536,1152]{1,0:T(8,128)(2,1)}), bf16[1536,1152]{1,0:T(8,128)(2,1)}) %all-reduce.10.cloned.1.call-update) | async-done | bytes 3538960 | tf_op jit(solution)/shard_map/psum | solution.py:164
  285.4 7.5 %fusion.60 = (f32[1536]{0:T(1024)S(1)}, f32[1536]{0:T(1024)S(1)}) fusion(f32[1536,6912]{1,0:T(8,128)} %bitcast.168, bf16[1536,1152]{1,0:T(8,128)(2,1)} %all-reduce.10.cloned.1.call-done, f32[1536]{0:T(1024)S(1)} %add_rsqrt_fusion, f32[1536,1152]{1,0:T(8,128)} %copy-done.2, f32[1536]{0:T(1024)S(1)} %broadcast_multiply_fusion.5), kind=kLoop, calls=%fused_computation.111 | loop fusion | flops 14152704 | bytes 17719296 | tf_op jit(solution)/shard_map/reduce_sum | solution.py:21
  293.5 12.1 %fusion.115 = (bf16[1152]{0:T(1024)(128)(2,1)S(1)}, bf16[1536,1152]{1,0:T(8,128)(2,1)S(1)}, f32[1536,1152]{1,0:T(8,128)}) fusion(f32[1536,6912]{1,0:T(8,128)} %bitcast.169, f32[1536]{0:T(1024)S(1)} %broadcast_multiply_fusion.3, f32[1536,1152]{1,0:T(8,128)} %copy-done.2, f32[1536]{0:T(1024)S(1)} %broadcast_multiply_fusion.5, ...), kind=kLoop, calls=%fused_computation.184 | loop fusion | flops 26540928 | bytes 38961408 | tf_op jit(solution)/shard_map/reduce_sum | solution.py:170
  321.6 5.3 fusion
  328.4 5.7 convolution_convert_fusion.4
  334.1 4.2 convolution_convert_fusion.5
  343.4 96.8 %all-reduce.12.cloned.1.call-done = (bf16[1536,1152]{1,0:T(8,128)(2,1)}, bf16[1536,1152]{1,0:T(8,128)(2,1)}) async-done(((bf16[1536,1152]{1,0:T(8,128)(2,1)}, bf16[1536,1152]{1,0:T(8,128)(2,1)}), (bf16[1536,1152]{1,0:T(8,128)(2,1)}, bf16[1536,1152]{1,0:T(8,128)(2,1)})) %all-reduce.12.cloned.1.call-update) | async-done | bytes 7077904 | tf_op jit(solution)/shard_map/psum | solution.py:144
  440.2 7.8 %fusion.61 = (f32[1536]{0:T(1024)S(1)}, f32[1536]{0:T(1024)S(1)}) fusion(f32[1536,6912]{1,0:T(8,128)} %bitcast.170, bf16[1536,1152]{1,0:T(8,128)(2,1)} %get-tuple-element.20, f32[1536]{0:T(1024)S(1)} %rsqrt.20, f32[1536]{0:T(1024)S(1)} %div.40, f32[1536]{0:T(1024)S(1)} %reshape.280, bf16[1536,1152]{1,0:T(8,128)(2,1)} %gather_fusion, ...), kind=kLoop, calls=%fused_computation.112 | loop fusion | flops 19461120 | bytes 14188032 | tf_op jit(solution)/shard_map/reduce_sum | solution.py:21
  451.6 17.0 %multiply_add_fusion = (f32[1536,1152]{1,0:T(8,128)}, bf16[1536,1152]{1,0:T(8,128)(2,1)}, f32[1536,6912]{1,0:T(8,128)}) fusion(f32[1536,1152]{1,0:T(8,128)} %get-tuple-element.38, f32[1536]{0:T(1024)S(1)} %broadcast_multiply_fusion.1, f32[1536]{0:T(1024)S(1)} %broadcast_multiply_fusion.2, f32[1536]{0:T(1024)S(1)} %rsqrt.20, f32[1536]{0:T(1024)S(1)} %div.40, ...), kind=kLoop, calls=%fused_computation.28 | loop fusion | flops 35389440 | bytes 56659968 | tf_op jit(solution)/shard_map/add | solution.py:220
  468.6 7.7 %multiply_dynamic-update-slice_fusion = f32[1536,6912]{1,0:T(8,128)} fusion(f32[1536,6912]{1,0:T(8,128)} %get-tuple-element.43, f32[1536,1152]{1,0:T(8,128)} %get-tuple-element.38, bf16[1536,1152]{1,0:T(8,128)(2,1)} %all-reduce.8.cloned.1.call-done, f32[1152]{0:T(1024)S(1)} %convert_element_type.251), kind=kLoop, calls=%fused_computation.27 | loop fusion | flops 5308416 | bytes 17699328
  479.6 4.2 fusion.1
  489.3 14.7 %reduce_sum.177 = f32[8,6912]{1,0:T(8,128)S(1)} reduce(f32[8,192,6912]{2,1,0:T(8,128)} %bitcast.176, f32[]{:T(128)} %constant.29.clone.1), dimensions={1}, to_apply=%region_29.30 | reduce | flops 10561536 | bytes 42688516 | tf_op jit(solution)/shard_map/reduce_sum | solution.py:232
  507.9 5.1 fusion.26
  513.0 5.6 fusion.53
  521.3 5.6 convolution_bitcast_fusion.2
  527.6 25.0 %all-reduce.1 = (bf16[2,144]{1,0:T(2,128)(2,1)S(1)}, bf16[1152]{0:T(1024)(128)(2,1)S(1)}, bf16[576]{0:T(1024)(128)(2,1)S(1)}, bf16[1152]{0:T(1024)(128)(2,1)S(1)...) all-reduce(bf16[2,144]{1,0:T(2,128)(2,1)S(1)} %pad_maximum_fusion, ...), channel_id=1, replica_groups=mesh['dp'=4,'mp'=8] {'dp'}, use_global_device_ids=true, to_apply=%region_19.20 | all-reduce | flops 5954 | bytes 23816 | tf_op jit(solution)/shard_map/psum | solution.py:260
  556.2 6.5 broadcast_multiply_fusion
  562.7 19.8 %scatter_custom_fusion = f32[2048,1152]{1,0:T(8,128)} fusion(s32[1536]{0:T(1024)S(1)} %reshape.288, f32[1536,1152]{1,0:T(8,128)} %bitcast.180, f32[]{:T(128)} %constant.29.clone.1), kind=kCustom, calls=%fused_computation.45 | custom fusion | flops 1769472 | bytes 9437696
  582.5 140.1 %all-reduce.14.cloned.1.call-done = (bf16[3,1152,144]{1,2,0:T(8,128)(2,1)}, bf16[144,1152]{1,0:T(8,128)(2,1)}, bf16[1152,576]{0,1:T(8,128)(2,1)}, bf16[576,1152]{1,0:T(8,128)(2,1)}, bf16[1152,864]{0,1:T(8,128)(2,1)}) async-done(((bf16[3,1152,144]{1,2,0:T(8,128)(2,1)}, bf16[144,1152]{1,0:T(8,128)(2,1)}, bf16[1152,576]{0,1:T(8,128)(2,1)}, bf16[576,1152]{1,0:T(8,128)(2,1)}, bf16[1152,864]{0,1:T(8,128)(2,1)}), ...) | async-done | bytes 5971984 | tf_op jit(solution)/shard_map/psum | solution.py:259
  (219 shorter events, 96.9 us)
Async XLA Ops:
  7.2 40.4 %copy-start = (bf16[1152,864]{0,1:T(8,128)(2,1)S(1)}, bf16[1152,864]{0,1:T(8,128)(2,1)}, u32[]{:S(2)}) copy-start(bf16[1152,864]{0,1:T(8,128)(2,1)} %param.29) | copy-start | bytes 5971972
  7.2 176.8 %all-reduce.8.cloned.1.call-start = ((), (), s32[]{:S(2)}) async-start(), calls=%async_computation | async-start | bytes 7077888 | tf_op jit(solution)/shard_map/psum | solution.py:130
  7.3 76.7 %copy-start.31 = (s32[16,16]{1,0:T(8,128)}, s32[16,16]{1,0:T(8,128)S(1)}, u32[]{:S(2)}) copy-start(s32[16,16]{1,0:T(8,128)S(1)} %subtract_add_fusion) | copy-start | bytes 3076
  9.4 84.8 %copy-start.35 = (s32[8,192]{1,0:T(8,128)}, s32[8,192]{1,0:T(8,128)S(1)}, u32[]{:S(2)}) copy-start(s32[8,192]{1,0:T(8,128)S(1)} %get-tuple-element.47) | copy-start | bytes 18436
  10.3 83.9 %copy-start.28 = (f32[8,192]{1,0:T(8,128)}, f32[8,192]{1,0:T(8,128)S(1)}, u32[]{:S(2)}) copy-start(f32[8,192]{1,0:T(8,128)S(1)} %get-tuple-element.49) | copy-start | bytes 18436
  42.6 4.9 copy-start.44
  42.6 5.0 copy-start.38
  59.3 14.3 %copy-start.4 = (bf16[1536,1152]{1,0:T(8,128)(2,1)S(1)}, bf16[1536,1152]{1,0:T(8,128)(2,1)}, u32[]{:S(2)}) copy-start(bf16[1536,1152]{1,0:T(8,128)(2,1)} %gather_fusion) | copy-start | bytes 10616836
  73.6 6.8 copy-start.51
  99.4 5.5 copy-start.17
  109.7 175.6 %all-reduce.10.cloned.1.call-start = ((), (), s32[]{:S(2)}) async-start(), calls=%async_computation.1 | async-start | bytes 7077888 | tf_op jit(solution)/shard_map/psum | solution.py:164
  109.8 7.2 copy-start.50
  193.5 6.1 copy-start.49
  193.5 6.5 copy-start.52
  199.9 5.6 copy-start.23
  211.4 228.8 %all-reduce.12.cloned.1.call-start = ((), (), s32[]{:S(2)}) async-start(), calls=%async_computation.2 | async-start | bytes 14155776 | tf_op jit(solution)/shard_map/psum | solution.py:144
  285.4 7.6 %copy-start.8 = (bf16[1536,1152]{1,0:T(8,128)(2,1)S(1)}, bf16[1536,1152]{1,0:T(8,128)(2,1)}, u32[]{:S(2)}) copy-start(bf16[1536,1152]{1,0:T(8,128)(2,1)} %all-reduce.10.cloned.1.call-done) | copy-start | bytes 10616836
  285.4 8.2 %copy-start.11 = (bf16[8,192,1152]{2,1,0:T(8,128)(2,1)S(1)}, bf16[8,192,1152]{2,1,0:T(8,128)(2,1)}, u32[]{:S(2)}) copy-start(bf16[8,192,1152]{2,1,0:T(8,128)(2,1)} %param.20) | copy-start | bytes 10616836
  327.0 395.7 %all-reduce.14.cloned.1.call-start = ((), (), s32[]{:S(2)}) async-start(), calls=%async_computation.3 | async-start | bytes 11943936 | tf_op jit(solution)/shard_map/psum | solution.py:259
  328.4 5.7 copy-start.20
  328.4 5.7 copy-start.53
  334.1 5.7 copy-start.34
  440.2 11.3 %slice-start = ((s8[7077888]{0:T(1024)(128)(4,1)}), s8[4194304]{0:T(1024)(128)(4,1)S(1)}, s32[]{:S(2)}) async-start(s8[7077888]{0:T(1024)(128)(4,1)} %bitcast.172), calls=%async_computation.4 | async-start | bytes 8388608
  440.2 7.9 %copy-start.13 = (bf16[1536,1152]{1,0:T(8,128)(2,1)S(1)}, bf16[1536,1152]{1,0:T(8,128)(2,1)}, u32[]{:S(2)}) copy-start(bf16[1536,1152]{1,0:T(8,128)(2,1)} %get-tuple-element.20) | copy-start | bytes 10616836
  440.2 11.3 %slice-start.1 = ((s8[7077888]{0:T(1024)(128)(4,1)}), s8[2883584]{0:T(1024)(128)(4,1)S(1)}, s32[]{:S(2)}) async-start(s8[7077888]{0:T(1024)(128)(4,1)} %bitcast.172), calls=%async_computation.5 | async-start | bytes 5767168
  468.6 7.7 %copy-start.9 = (bf16[1536,1152]{1,0:T(8,128)(2,1)S(1)}, bf16[1536,1152]{1,0:T(8,128)(2,1)}, u32[]{:S(2)}) copy-start(bf16[1536,1152]{1,0:T(8,128)(2,1)} %all-reduce.10.cloned.1.call-done) | copy-start | bytes 10616836
  479.6 5.6 copy-start.16
  489.3 14.7 %copy-start.39 = (bf16[8,1152]{1,0:T(8,128)(2,1)S(1)}, bf16[8,1152]{1,0:T(8,128)(2,1)}, u32[]{:S(2)}) copy-start(bf16[8,1152]{1,0:T(8,128)(2,1)} %param.17) | copy-start | bytes 55300
  513.0 8.3 %copy-start.32 = (s32[16,16]{1,0:T(8,128)S(1)}, s32[16,16]{1,0:T(8,128)}, u32[]{:S(2)}) copy-start(s32[16,16]{1,0:T(8,128)} %copy-done.31) | copy-start | bytes 3076
  521.3 6.3 copy-start.40
  722.7 4.7 copy-start.27
  724.6 4.4 copy-start.26
  (30 other events, 70.4 us)
Sparse Core Ops, SparseCore 0:
  109.8 74.0 all-reduce.7
  211.5 73.7 all-reduce.9
  327.1 113.1 all-reduce.11
  507.4 215.2 all-reduce.13
where the time goes:
time: 745 us; the launch traced here: 740 us
  waiting for transfers between devices  366 us (49%)
  other arithmetic  157 us (21%)
  matrix products  90.9 us (12%)
  local copies, waits for them, and re-layouts  75 us (10%)
  blocking collectives  35.8 us (5%)
  between operations  15 us (2%)
    psum x1, waiting for transfers between devices, body(): lax.psum(project_grad.astype(jnp.bfloat16), 'dp').astype(jnp.float32)  140 us
    psum x1, waiting for transfers between devices, body(): lax.psum(jnp.dot(activated_hidden, down_weight, preferred_element_type=jn...  96.8 us
    psum x1, waiting for transfers between devices, body(): lax.psum(times_transposed(d_pre, up_weight).astype(jnp.bfloat16), 'mp')  65.9 us
    psum x1, waiting for transfers between devices, body(): lax.psum(jnp.dot(attended_values, merge_weight, preferred_element_type=jn...  62.6 us
    unnamed x9, other arithmetic  38.7 us
    gather x3, local copies, waits for them, and re-layouts, body(): jnp.take_along_axis(patches, positions[:, :, None], axis=1)  32.3 us
    psum x1, blocking collectives, body(): lax.psum(project_bias_grad.astype(jnp.bfloat16), 'dp').astype(jnp.float32)  25 us
    add x1, other arithmetic, body(): d_hidden_one + layer_back(d_attn_in * (1.0 + scale_one), normed_one, inv_...  17 us
  transfers between devices with their start and end apart: 4, of which 4 were waited for; matrix products, arithmetic and copies ran while one was open for 11% of the time, Pallas kernels for 0%

commit v1 on v0

--- a/solution.py
+++ b/solution.py
@@ -161,9 +161,9 @@
     d_pre = gelu_pull(d_act)[0].astype(jnp.bfloat16)
     up_grad = transposed_times(mlp_own, d_pre)
     up_bias_grad = jnp.sum(d_pre.astype(jnp.float32), axis=0)
-    d_mlp_in = lax.psum(times_transposed(d_pre, up_weight).astype(jnp.bfloat16), "mp").astype(
-        jnp.float32
-    )
+    d_mlp_in = jnp.sum(
+        lax.all_gather(times_transposed(d_pre, up_weight).astype(jnp.bfloat16), "mp"), axis=0
+    ).astype(jnp.float32)
     d_hidden_one = d_out + layer_back(d_mlp_in * (1.0 + scale_two), normed_two, inv_two)
     d_attn_own = (gate_one * d_hidden_one).astype(jnp.bfloat16)
     merge_grad = transposed_times(attended_values, d_attn_own)

time: 745 us -> 823 us (1.10)
  waiting for transfers between devices: 366 us -> 430 us
  other arithmetic: 157 us -> 171 us
    all_gather x0 -> x1, waiting for transfers between devices: none -> 131 us  [body(): lax.all_gather(times_transposed(d_pre, up_weight).astype(jnp.bfloat16), '...]
    psum x1 -> x0, waiting for transfers between devices: 65.9 us -> none  [body(): lax.psum(times_transposed(d_pre, up_weight).astype(jnp.bfloat16), 'mp')]
    reduce_sum x0 -> x1, other arithmetic: none -> 12.4 us  [body(): jnp.sum(lax.all_gather(times_transposed(d_pre, up_weight).astype(jnp.bflo...]
  transfers between devices with their start and end apart: 4 -> 4, of which waited for: 4 -> 4; matrix products, arithmetic and copies ran while one was open for 11% -> 10% of each run, Pallas kernels for 0% -> 0%
where the time goes in v1:
time: 823 us; the launch traced here: 818 us
  waiting for transfers between devices  430 us (52%)
  other arithmetic  171 us (21%)
  matrix products  91.4 us (11%)
  local copies, waits for them, and re-layouts  74.8 us (9%)
  blocking collectives  35.8 us (4%)
  between operations  14.8 us (2%)
    psum x1, waiting for transfers between devices, body(): lax.psum(project_grad.astype(jnp.bfloat16), 'dp').astype(jnp.float32)  140 us
    all_gather x1, waiting for transfers between devices, body(): lax.all_gather(times_transposed(d_pre, up_weight).astype(jnp.bfloat16), '...  131 us
    psum x1, waiting for transfers between devices, body(): lax.psum(jnp.dot(activated_hidden, down_weight, preferred_element_type=jn...  96.8 us
    psum x1, waiting for transfers between devices, body(): lax.psum(jnp.dot(attended_values, merge_weight, preferred_element_type=jn...  62.5 us
    unnamed x9, other arithmetic  38.7 us
    gather x3, local copies, waits for them, and re-layouts, body(): jnp.take_along_axis(patches, positions[:, :, None], axis=1)  32.3 us
    psum x1, blocking collectives, body(): lax.psum(project_bias_grad.astype(jnp.bfloat16), 'dp').astype(jnp.float32)  25.1 us
    add x1, other arithmetic, body(): d_hidden_one + layer_back(d_attn_in * (1.0 + scale_one), normed_one, inv_...  17 us
  transfers between devices with their start and end apart: 4, of which 4 were waited for; matrix products, arithmetic and copies ran while one was open for 10% of the time, Pallas kernels for 0%

profile of v1, /device:TPU:0, one launch (start us, length us, event | category | flops | bytes accessed | tf_op | source)
XLA Modules:
  0.0 818.2 jit_solution(10925066622737210936)
XLA Ops:
  10.4 32.2 %gather_fusion = bf16[1536,1152]{1,0:T(8,128)(2,1)} fusion(bf16[8,256,1152]{2,1,0:T(8,128)(2,1)} %param.16, s32[1536]{0:T(1024)S(1)} %reshape.282), kind=kCustom, calls=%fused_computation | custom fusion | bytes 7090176 | tf_op jit(solution)/shard_map/jit(take_along_axis)/gather | solution.py:92
  48.2 10.8 %all-gather.1 = f32[8,864,8]{1,2,0:T(8,128)S(1)} all-gather(f32[1,864,8]{1,2,0:T(8,128)S(1)} %fusion.58), channel_id=1, replica_groups=mesh['dp'=4,'mp'=8] {'mp'}, dimensions={0}, use_global_device_ids=true | all-gather | bytes 248832 | tf_op jit(solution)/shard_map/all_gather | solution.py:85
  59.3 14.1 %broadcast_in_dim.39 = f32[8,192,6912]{2,1,0:T(8,128)} broadcast(f32[8,6912]{1,0:T(8,128)S(1)} %bitcast.186), dimensions={0,2} | broadcast | bytes 42688512 | tf_op jit(solution)/shard_map/broadcast_in_dim | solution.py:86
  73.3 6.7 fusion.4
  93.9 4.4 fusion.24
  109.9 5.5 fusion.111
  117.3 4.3 fusion.123
  121.6 62.5 %all-reduce.7.cloned.1.call-done = bf16[1536,1152]{1,0:T(8,128)(2,1)} async-done(((bf16[1536,1152]{1,0:T(8,128)(2,1)}), bf16[1536,1152]{1,0:T(8,128)(2,1)}) %all-reduce.7.cloned.1.call-update) | async-done | bytes 3538960 | tf_op jit(solution)/shard_map/psum | solution.py:130
  184.1 6.5 fusion.117
  193.5 6.1 fusion.3
  200.0 5.5 fusion.113
  206.8 4.7 convolution_convert_fusion.1
  211.7 7.9 convolution_convert_fusion.2
  219.6 130.7 %all-gather.4.cloned.1.call-done = bf16[12288,1152]{1,0:T(8,128)(2,1)} async-done(((bf16[1536,1152]{1,0:T(8,128)(2,1)}), bf16[12288,1152]{1,0:T(8,128)(2,1)}) %all-gather.4.cloned.1.call-update) | async-done | bytes 28311568 | tf_op jit(solution)/shard_map/all_gather | solution.py:165
  350.3 12.4 %reduce_sum.179 = bf16[1536,1152]{1,0:T(8,128)(2,1)} reduce(bf16[8,1536,1152]{2,1,0:T(8,128)(2,1)} %bitcast.179, bf16[]{:T(256)} %constant.73.clone.1), dimensions={0}, to_apply=%region_8.9 | reduce | flops 12386304 | bytes 31850498 | tf_op jit(solution)/shard_map/reduce_sum | solution.py:164
  362.7 7.5 fusion.60
  370.9 12.3 %fusion.115 = (bf16[1152]{0:T(1024)(128)(2,1)S(1)}, bf16[1536,1152]{1,0:T(8,128)(2,1)S(1)}, f32[1536,1152]{1,0:T(8,128)}) fusion(f32[1536,6912]{1,0:T(8,128)} %bitcast.170, f32[1536]{0:T(1024)S(1)} %broadcast_multiply_fusion.3, f32[1536,1152]{1,0:T(8,128)} %copy-done.2, f32[1536]{0:T(1024)S(1)} %broadcast_multiply_fusion.5, ...), kind=kLoop, calls=%fused_computation.184 | loop fusion | flops 26540928 | bytes 38961408 | tf_op jit(solution)/shard_map/reduce_sum | solution.py:170
  399.2 5.2 fusion
  405.9 5.7 convolution_convert_fusion.4
  420.9 96.8 %all-reduce.9.cloned.1.call-done = (bf16[1536,1152]{1,0:T(8,128)(2,1)}, bf16[1536,1152]{1,0:T(8,128)(2,1)}) async-done(((bf16[1536,1152]{1,0:T(8,128)(2,1)}, bf16[1536,1152]{1,0:T(8,128)(2,1)}), (bf16[1536,1152]{1,0:T(8,128)(2,1)}, bf16[1536,1152]{1,0:T(8,128)(2,1)})) %all-reduce.9.cloned.1.call-update) | async-done | bytes 7077904 | tf_op jit(solution)/shard_map/psum | solution.py:144
  517.7 8.8 %fusion.61 = (f32[1536]{0:T(1024)S(1)}, f32[1536]{0:T(1024)S(1)}) fusion(f32[1536,6912]{1,0:T(8,128)} %bitcast.171, bf16[1536,1152]{1,0:T(8,128)(2,1)} %get-tuple-element.20, f32[1536]{0:T(1024)S(1)} %rsqrt.20, f32[1536]{0:T(1024)S(1)} %div.40, f32[1536]{0:T(1024)S(1)} %reshape.280, bf16[1536,1152]{1,0:T(8,128)(2,1)} %gather_fusion, ...), kind=kLoop, calls=%fused_computation.112 | loop fusion | flops 19461120 | bytes 14188032 | tf_op jit(solution)/shard_map/reduce_sum | solution.py:21
  530.1 17.0 %multiply_add_fusion = (f32[1536,1152]{1,0:T(8,128)}, bf16[1536,1152]{1,0:T(8,128)(2,1)}, f32[1536,6912]{1,0:T(8,128)}) fusion(f32[1536,1152]{1,0:T(8,128)} %get-tuple-element.38, f32[1536]{0:T(1024)S(1)} %broadcast_multiply_fusion.1, f32[1536]{0:T(1024)S(1)} %broadcast_multiply_fusion.2, f32[1536]{0:T(1024)S(1)} %rsqrt.20, f32[1536]{0:T(1024)S(1)} %div.40, ...), kind=kLoop, calls=%fused_computation.28 | loop fusion | flops 35389440 | bytes 56659968 | tf_op jit(solution)/shard_map/add | solution.py:220
  547.0 7.7 multiply_dynamic-update-slice_fusion
  558.1 4.2 fusion.1
  567.8 14.7 %reduce_sum.190 = f32[8,6912]{1,0:T(8,128)S(1)} reduce(f32[8,192,6912]{2,1,0:T(8,128)} %bitcast.177, f32[]{:T(128)} %constant.30.clone.1), dimensions={1}, to_apply=%region_29.30 | reduce | flops 10561536 | bytes 42688516 | tf_op jit(solution)/shard_map/reduce_sum | solution.py:232
  586.4 5.1 fusion.26
  591.5 5.6 fusion.53
  599.7 5.6 convolution_bitcast_fusion.2
  606.0 25.1 %all-reduce.1 = (bf16[2,144]{1,0:T(2,128)(2,1)S(1)}, bf16[1152]{0:T(1024)(128)(2,1)S(1)}, bf16[576]{0:T(1024)(128)(2,1)S(1)}, bf16[1152]{0:T(1024)(128)(2,1)S(1)...) all-reduce(bf16[2,144]{1,0:T(2,128)(2,1)S(1)} %pad_maximum_fusion, ...), channel_id=1, replica_groups=mesh['dp'=4,'mp'=8] {'dp'}, use_global_device_ids=true, to_apply=%region_19.20 | all-reduce | flops 5954 | bytes 23816 | tf_op jit(solution)/shard_map/psum | solution.py:260
  634.7 6.5 broadcast_multiply_fusion
  641.1 19.8 %scatter_custom_fusion = f32[2048,1152]{1,0:T(8,128)} fusion(s32[1536]{0:T(1024)S(1)} %reshape.288, f32[1536,1152]{1,0:T(8,128)} %bitcast.182, f32[]{:T(128)} %constant.30.clone.1), kind=kCustom, calls=%fused_computation.45 | custom fusion | flops 1769472 | bytes 9437696
  661.0 140.2 %all-reduce.11.cloned.1.call-done = (bf16[3,1152,144]{1,2,0:T(8,128)(2,1)}, bf16[144,1152]{1,0:T(8,128)(2,1)}, bf16[1152,576]{0,1:T(8,128)(2,1)}, bf16[576,1152]{1,0:T(8,128)(2,1)}, bf16[1152,864]{0,1:T(8,128)(2,1)}) async-done(((bf16[3,1152,144]{1,2,0:T(8,128)(2,1)}, bf16[144,1152]{1,0:T(8,128)(2,1)}, bf16[1152,576]{0,1:T(8,128)(2,1)}, bf16[576,1152]{1,0:T(8,128)(2,1)}, bf16[1152,864]{0,1:T(8,128)(2,1)}), ...) | async-done | bytes 5971984 | tf_op jit(solution)/shard_map/psum | solution.py:259
  (220 shorter events, 101.4 us)
Async XLA Ops:
  7.2 40.4 %copy-start = (bf16[1152,864]{0,1:T(8,128)(2,1)S(1)}, bf16[1152,864]{0,1:T(8,128)(2,1)}, u32[]{:S(2)}) copy-start(bf16[1152,864]{0,1:T(8,128)(2,1)} %param.29) | copy-start | bytes 5971972
  7.2 176.9 %all-reduce.7.cloned.1.call-start = ((), (), s32[]{:S(2)}) async-start(), calls=%async_computation | async-start | bytes 7077888 | tf_op jit(solution)/shard_map/psum | solution.py:130
  7.3 76.4 %copy-start.31 = (s32[16,16]{1,0:T(8,128)}, s32[16,16]{1,0:T(8,128)S(1)}, u32[]{:S(2)}) copy-start(s32[16,16]{1,0:T(8,128)S(1)} %subtract_add_fusion) | copy-start | bytes 3076
  9.4 84.5 %copy-start.35 = (s32[8,192]{1,0:T(8,128)}, s32[8,192]{1,0:T(8,128)S(1)}, u32[]{:S(2)}) copy-start(s32[8,192]{1,0:T(8,128)S(1)} %get-tuple-element.47) | copy-start | bytes 18436
  10.3 83.7 %copy-start.28 = (f32[8,192]{1,0:T(8,128)}, f32[8,192]{1,0:T(8,128)S(1)}, u32[]{:S(2)}) copy-start(f32[8,192]{1,0:T(8,128)S(1)} %get-tuple-element.49) | copy-start | bytes 18436
  42.6 4.9 copy-start.44
  42.6 5.0 copy-start.38
  59.3 14.1 %copy-start.4 = (bf16[1536,1152]{1,0:T(8,128)(2,1)S(1)}, bf16[1536,1152]{1,0:T(8,128)(2,1)}, u32[]{:S(2)}) copy-start(bf16[1536,1152]{1,0:T(8,128)(2,1)} %gather_fusion) | copy-start | bytes 10616836
  73.3 6.8 copy-start.51
  99.1 5.8 copy-start.17
  109.8 240.5 %all-gather.4.cloned.1.call-start = ((), (), s32[]{:S(2)}) async-start(), calls=%async_computation.1 | async-start | bytes 31850496 | tf_op jit(solution)/shard_map/all_gather | solution.py:165
  109.9 7.4 copy-start.50
  193.5 6.1 copy-start.49
  193.5 6.5 copy-start.52
  200.0 5.5 copy-start.23
  211.5 306.2 %all-reduce.9.cloned.1.call-start = ((), (), s32[]{:S(2)}) async-start(), calls=%async_computation.2 | async-start | bytes 14155776 | tf_op jit(solution)/shard_map/psum | solution.py:144
  362.7 7.6 copy-start.6
  362.7 8.2 copy-start.11
  404.5 396.7 %all-reduce.11.cloned.1.call-start = ((), (), s32[]{:S(2)}) async-start(), calls=%async_computation.3 | async-start | bytes 11943936 | tf_op jit(solution)/shard_map/psum | solution.py:259
  405.9 5.7 copy-start.20
  405.9 5.7 copy-start.53
  411.6 5.7 copy-start.34
  517.7 12.4 %slice-start = ((s8[7077888]{0:T(1024)(128)(4,1)}), s8[4194304]{0:T(1024)(128)(4,1)S(1)}, s32[]{:S(2)}) async-start(s8[7077888]{0:T(1024)(128)(4,1)} %bitcast.173), calls=%async_computation.4 | async-start | bytes 8388608
  517.7 8.8 %copy-start.13 = (bf16[1536,1152]{1,0:T(8,128)(2,1)S(1)}, bf16[1536,1152]{1,0:T(8,128)(2,1)}, u32[]{:S(2)}) copy-start(bf16[1536,1152]{1,0:T(8,128)(2,1)} %get-tuple-element.20) | copy-start | bytes 10616836
  517.7 12.4 %slice-start.1 = ((s8[7077888]{0:T(1024)(128)(4,1)}), s8[2883584]{0:T(1024)(128)(4,1)S(1)}, s32[]{:S(2)}) async-start(s8[7077888]{0:T(1024)(128)(4,1)} %bitcast.173), calls=%async_computation.5 | async-start | bytes 5767168
  547.0 7.7 copy-start.7
  558.1 5.6 copy-start.16
  567.8 14.7 %copy-start.39 = (bf16[8,1152]{1,0:T(8,128)(2,1)S(1)}, bf16[8,1152]{1,0:T(8,128)(2,1)}, u32[]{:S(2)}) copy-start(bf16[8,1152]{1,0:T(8,128)(2,1)} %param.17) | copy-start | bytes 55300
  591.5 8.3 %copy-start.32 = (s32[16,16]{1,0:T(8,128)S(1)}, s32[16,16]{1,0:T(8,128)}, u32[]{:S(2)}) copy-start(s32[16,16]{1,0:T(8,128)} %copy-done.31) | copy-start | bytes 3076
  599.7 6.3 copy-start.40
  801.1 4.7 copy-start.27
  803.1 4.4 copy-start.26
  (30 other events, 70.5 us)
Sparse Core Ops, SparseCore 0:
  109.9 74.0 all-reduce.6
  211.6 138.6 all-gather.3
  404.6 113.0 all-reduce.8
  585.8 215.2 all-reduce.10
